TPU v7x, 32 devices: a whole 2x2x4 slice. The times are simulated.
32 devices in a mesh: tg: 2 (over core), pw: 16 (over z, y, x).
Axes of the slice: x: 2, y: 2, z: 4, core: 2. Of those that a mesh axis runs over, the one named last changes fastest.
Arguments:
- coeffs: float32 [2, 8192, 256], P(None, ('tg', 'pw')), may hold values from -6 to 6
- g_place: int32 [8192], P(('tg', 'pw')), may hold values from 0 to 2047, as said below
- stick_column: int32 [512], P(('tg', 'pw')), may hold values from 0 to 16383, as said below
- potential: float32 [128, 128, 128], P(None, None, ('tg', 'pw')), may hold values from -1 to 3
Outputs:
- hpsi: float32 [2, 8192, 256], P(None, ('tg', 'pw'))
Inputs may be any that keep to these rules, and one draw needn't show every extreme that they name: g_place[g] = s * 128 + z: s is a stick slot of the owner g // 256, z a frequency within 32 of zero taken modulo 128; no two plane waves of one owner share s and z; each owner uses its slots 0 up to some count between 4 and 16, every one of them, and some owner uses all 16. `stick_column`: all stick slots name different columns x * 128 + y; with x and y read as signed frequencies (taken modulo 128), x * x + y * y <= 32 ** 2.
All inputs are finite; a program needn't handle non-finite values.
Results may differ from a plain program's by a relative error of at most 0.009.
Values may be sent and summed in bfloat16 or wider, within the bound.
A program may use at most 256 MiB of HBM per device.

v0:
```python
import jax
import jax.numpy as jnp
from jax import lax
from jax.sharding import PartitionSpec as P

NR = 128
ZSPAN = 64


def phase_table(left_index, right_index, sign_value, modulus):
    product = left_index[:, None] * right_index[None, :] % modulus
    angles = 2.0 * jnp.pi / modulus * product.astype(jnp.float32)
    cosine = jnp.cos(angles)
    sine_part = sign_value * jnp.sin(angles)
    upper_row = jnp.stack([cosine, sine_part])
    lower_row = jnp.stack([-sine_part, cosine])
    return jnp.stack([upper_row, lower_row])


def box_selectors(column_order):
    half_span = ZSPAN // 2
    box_side = ZSPAN + 1
    x_index = column_order // NR
    y_index = column_order % NR
    x_box = jnp.where(x_index > NR // 2, x_index - NR, x_index) + half_span
    y_box = jnp.where(y_index > NR // 2, y_index - NR, y_index) + half_span
    cells = jnp.arange(box_side * box_side, dtype=jnp.int32)
    forward_select = (cells[:, None] == (y_box * box_side + x_box)[None, :]).astype(jnp.bfloat16)
    backward_select = (cells[:, None] == (x_box * box_side + y_box)[None, :]).astype(jnp.bfloat16)
    return (forward_select, backward_select)


def box_tables():
    box_side = ZSPAN + 1
    frequency = jnp.arange(NR, dtype=jnp.int32)
    box_freq = jnp.mod(jnp.arange(box_side, dtype=jnp.int32) - ZSPAN // 2, NR)
    ahead = phase_table(box_freq, frequency, 1.0, NR).astype(jnp.bfloat16)
    behind = phase_table(frequency, box_freq, -1.0, NR).astype(jnp.bfloat16)
    return (ahead, behind)


def plane_pass(received, selectors, volume, ahead, behind):
    forward_select, backward_select = selectors
    box_side = ZSPAN + 1
    plane_count = received.shape[2]
    band_count = received.shape[3]
    width = plane_count * band_count
    flat = received.reshape(2, received.shape[1], width)
    partial_value = None
    for part_index in range(2):
        lattice = jnp.dot(
            forward_select, flat[part_index], preferred_element_type=jnp.float32
        ).astype(jnp.bfloat16)
        lattice = lattice.reshape(box_side, box_side, width)
        term = jnp.einsum(
            "dyk,yxm->dkxm", ahead[part_index], lattice, preferred_element_type=jnp.float32
        )
        partial_value = term if partial_value is None else partial_value + term
    partial_value = partial_value.astype(jnp.bfloat16)
    psi_field = jnp.einsum(
        "cdxr,ckxm->drkm", ahead, partial_value, preferred_element_type=jnp.float32
    )
    psi_field = psi_field.reshape(2, NR, NR, plane_count, band_count) * volume[None, :, :, :, None]
    weighted = psi_field.reshape(2, NR, NR, width).astype(jnp.bfloat16)
    reverse_half = jnp.einsum(
        "cdyq,cxym->dqxm", behind, weighted, preferred_element_type=jnp.float32
    ).astype(jnp.bfloat16)
    real_image = jnp.einsum(
        "cdxq,cyxm->dqym", behind, reverse_half, preferred_element_type=jnp.float32
    )
    boxed = real_image.astype(jnp.bfloat16).reshape(2, box_side * box_side, width)
    picked = jnp.stack(
        [
            jnp.einsum(
                "qs,qm->sm", backward_select, boxed[part_index], preferred_element_type=jnp.float32
            )
            for part_index in range(2)
        ]
    )
    return picked.astype(jnp.bfloat16).reshape(2, received.shape[1], plane_count, band_count)


def spread(shared, indices, slot_total):
    band_count = shared.shape[2]
    selector = (indices[:, None] == jnp.arange(slot_total * NR, dtype=jnp.int32)[None, :]).astype(
        jnp.float32
    )
    placed = jnp.einsum("gq,cgb->cqb", selector, shared, precision=lax.Precision.HIGHEST)
    return (selector, placed.reshape(2, slot_total, NR, band_count))


def ahead_sticks(placed, plane_of):
    frequency = jnp.arange(NR, dtype=jnp.int32)
    ahead_table = phase_table(frequency, plane_of, 1.0, NR)
    sticks = jnp.einsum("cszb,cdzk->dskb", placed, ahead_table, precision=lax.Precision.HIGHEST)
    return sticks.astype(jnp.bfloat16)


def finish(arrived, plane_of, selector):
    frequency = jnp.arange(NR, dtype=jnp.int32)
    return_table = phase_table(plane_of, frequency, -1.0, NR)
    spectra = jnp.einsum(
        "cszb,cdzk->dskb",
        arrived.astype(jnp.float32),
        return_table,
        precision=lax.Precision.HIGHEST,
    )
    band_count = arrived.shape[3]
    picked = jnp.einsum(
        "gq,cqb->cgb", selector, spectra.reshape(2, -1, band_count), precision=lax.Precision.HIGHEST
    )
    return picked * (1.0 / NR**3)


def body(coeffs, g_place, stick_column, potential):
    columns = lax.all_gather(stick_column, ("tg", "pw"), axis=0, tiled=True)
    ahead, behind = box_tables()
    slot_width = stick_column.shape[0]
    plane_of = jnp.arange(NR, dtype=jnp.int32)
    selector, placed = spread(coeffs, g_place, slot_width)
    sticks = ahead_sticks(placed, plane_of)
    selectors = box_selectors(columns)
    returned = plane_pass(
        lax.all_to_all(sticks, ("tg", "pw"), split_axis=2, concat_axis=1, tiled=True),
        selectors,
        potential,
        ahead,
        behind,
    )
    arrived = lax.all_to_all(returned, ("tg", "pw"), split_axis=1, concat_axis=2, tiled=True)
    return finish(arrived, plane_of, selector)


def solution(mesh):
    placed = (
        P(None, ("tg", "pw"), None),
        P(("tg", "pw")),
        P(("tg", "pw")),
        P(None, None, ("tg", "pw")),
    )
    return jax.shard_map(
        body, mesh=mesh, in_specs=placed, out_specs=P(None, ("tg", "pw"), None), check_vma=False
    )
```

profile of v0, /device:TPU:0, one launch (start us, length us, event | category | flops | bytes accessed | tf_op | source)
XLA Modules:
  0.0 620.8 jit_solution(15119981255612048079)
XLA Ops:
  10.8 7.3 %all-to-all-start = ((bf16[2,16,128,256]{3,1,0,2:T(8,128)(2,1)}), bf16[2,16,128,256]{3,1,0,2:T(8,128)(2,1)S(1)}, u32[]{:S(2)}, u32[]{:S(2)}) async-start(bf16[2,16,128,256]{3,1,0,2:T(8,128)(2,1)} %copy.34), calls=%async_computation | async-start | bytes 4194304 | tf_op jit(solution)/shard_map/all_to_all | solution.py:124
  18.1 7.6 %copy.40 = f32[128,128,4]{2,0,1:T(8,128)} copy(f32[128,128,4]{1,2,0:T(4,128)S(1)} %copy-done.7) | data formatting | bytes 524288 | tf_op args[3]
  25.7 24.4 %mul.358 = f32[128,128,4,256]{3,2,0,1:T(4,128)} broadcast(f32[128,128,4]{2,0,1:T(8,128)} %copy.40), dimensions={0,1,2} | broadcast | bytes 67371008 | tf_op jit(solution)/shard_map/mul | solution.py:63
  50.1 80.1 %mul.359 = f32[128,128,1024]{2,0,1:T(8,128)} reshape(f32[128,128,4,256]{3,2,0,1:T(4,128)} %mul.358) | data formatting | bytes 134217728 | tf_op jit(solution)/shard_map/mul | solution.py:63
  130.5 40.7 %all-reduce = s32[512]{0:T(512)S(1)} all-reduce(s32[512]{0:T(512)S(1)} %dynamic-update-slice), channel_id=1, replica_groups=mesh['tg'=2,'pw'=16] {'tg','pw'}, use_global_device_ids=true, to_apply=%add | all-reduce | flops 512 | bytes 4096
  177.0 7.0 %convolution_convert_fusion.1 = bf16[4225,1024]{1,0:T(8,128)(2,1)} fusion(bf16[512,1024]{1,0:T(8,128)(2,1)S(1)} %bitcast.182, s32[512]{0:T(512)S(1)} %get-tuple-element.18), kind=kOutput, calls=%fused_computation.19 | convolution fusion | flops 4436723200 | bytes 9703424 | tf_op jit(solution)/shard_map/dot_general | solution.py:51
  184.1 10.6 %reshape.430 = bf16[65,65,1024]{2,1,0:T(8,128)(2,1)} reshape(bf16[4225,1024]{1,0:T(8,128)(2,1)} %convolution_convert_fusion.1) | data formatting | bytes 17305600 | tf_op jit(solution)/shard_map/reshape | solution.py:54
  194.6 31.5 %fusion.14 = f32[2,128,65,1024]{3,1,2,0:T(8,128)} fusion(bf16[65,65,1024]{2,1,0:T(8,128)(2,1)} %reshape.430, bf16[1,65,128]{2,1,0:T(8,128)(2,1)S(1)} %get-tuple-element.23, bf16[1,65,128]{2,1,0:T(8,128)(2,1)S(1)} %get-tuple-element.24), kind=kOutput, calls=%fused_computation.14 | convolution fusion | flops 2215183360 | bytes 76843520 | tf_op jit(solution)/shard_map/dyk,yxm->dkxm/dot_general | solution.py:55
  226.4 7.0 %convolution_convert_fusion = bf16[4225,1024]{1,0:T(8,128)(2,1)} fusion(bf16[512,1024]{1,0:T(8,128)(2,1)S(1)} %bitcast.181, s32[512]{0:T(512)S(1)} %get-tuple-element.18), kind=kOutput, calls=%fused_computation.18 | convolution fusion | flops 4436723200 | bytes 9703424 | tf_op jit(solution)/shard_map/dot_general | solution.py:51
  233.4 10.5 %reshape.431 = bf16[65,65,1024]{2,1,0:T(8,128)(2,1)} reshape(bf16[4225,1024]{1,0:T(8,128)(2,1)} %convolution_convert_fusion) | data formatting | bytes 17305600 | tf_op jit(solution)/shard_map/reshape | solution.py:54
  243.9 49.8 %add_convert_fusion = bf16[2,128,65,1024]{3,1,2,0:T(8,128)(2,1)} fusion(f32[2,128,65,1024]{3,1,2,0:T(8,128)} %fusion.14, bf16[65,65,1024]{2,1,0:T(8,128)(2,1)} %reshape.431, bf16[1,65,128]{2,1,0:T(8,128)(2,1)S(1)} %get-tuple-element.24, bf16[1,65,128]{2,1,0:T(8,128)(2,1)S(1)} %get-tuple-element.22), kind=kOutput, calls=%fused_computation.3 | convolution fusion | flops 2249262080 | bytes 110922240 | tf_op jit(solution)/shard_map/dyk,yxm->dkxm/dot_general | solution.py:55
  293.7 70.8 %fusion = bf16[2,128,128,1024]{3,1,2,0:T(8,128)(2,1)} fusion(f32[128,128,1024]{2,0,1:T(8,128)} %mul.359, bf16[2,128,65,1024]{3,1,2,0:T(8,128)(2,1)} %add_convert_fusion, bf16[1,2,65,128]{3,2,1,0:T(8,128)(2,1)S(1)} %get-tuple-element.16, bf16[1,2,65,128]{3,2,1,0:T(8,128)(2,1)S(1)} %get-tuple-element.15), kind=kOutput, calls=%fused_computation.1 | convolution fusion | flops 8791293952 | bytes 168363008 | tf_op jit(solution)/shard_map/cdxr,ckxm->drkm/dot_general | solution.py:60
  364.5 65.0 %bitcast_convert_fusion = bf16[2,65,128,1024]{3,1,2,0:T(8,128)(2,1)} fusion(bf16[2,128,128,1024]{3,1,2,0:T(8,128)(2,1)} %fusion, bf16[1,2,128,65]{2,3,0,1:T(8,128)(2,1)S(1)} %copy-done.6, bf16[1,2,128,65]{2,3,0,1:T(8,128)(2,1)S(1)} %copy-done.5), kind=kOutput, calls=%fused_computation.2 | convolution fusion | flops 8741324800 | bytes 101254144 | tf_op jit(solution)/shard_map/cdyq,cxym->dqxm/dot_general | solution.py:65
  429.4 24.8 %bitcast_convert_fusion.1 = bf16[2,65,65,1024]{3,1,2,0:T(8,128)(2,1)} fusion(bf16[2,65,128,1024]{3,1,2,0:T(8,128)(2,1)} %bitcast_convert_fusion, bf16[1,2,128,65]{2,3,0,1:T(8,128)(2,1)S(1)} %copy-done.6, bf16[1,2,128,65]{2,3,0,1:T(8,128)(2,1)S(1)} %copy-done.5), kind=kOutput, calls=%fused_computation.7 | convolution fusion | flops 4439019520 | bytes 51450880 | tf_op jit(solution)/shard_map/cdxq,cyxm->dqym/dot_general | solution.py:68
  454.2 15.1 %fusion.106 = (bf16[1,65,65,1024]{3,1,2,0:T(8,128)(2,1)}, bf16[1,65,65,1024]{3,1,2,0:T(8,128)(2,1)}) fusion(bf16[2,65,65,1024]{3,1,2,0:T(8,128)(2,1)} %bitcast_convert_fusion.1), kind=kLoop, calls=%fused_computation.138 | loop fusion | bytes 34611200 | tf_op jit(solution)/shard_map/slice | solution.py:75
  469.3 12.5 %copy.43 = bf16[1,65,65,1024]{3,2,1,0:T(8,128)(2,1)} copy(bf16[1,65,65,1024]{3,1,2,0:T(8,128)(2,1)} %get-tuple-element.5) | data formatting | bytes 17305600 | tf_op jit(solution)/shard_map/slice | solution.py:75
  481.8 10.5 %squeeze.16 = bf16[4225,1024]{1,0:T(8,128)(2,1)} reshape(bf16[1,65,65,1024]{3,2,1,0:T(8,128)(2,1)} %copy.43) | data formatting | bytes 17305600 | tf_op jit(solution)/shard_map/squeeze | solution.py:75
  492.3 11.9 %copy.44 = bf16[1024,4225]{1,0:T(8,128)(2,1)} copy(bf16[1024,4225]{0,1:T(8,128)(2,1)} %bitcast.169) | data formatting | bytes 17305600 | tf_op jit(solution)/shard_map/qs,qm->sm/dot_general | solution.py:74
  504.2 12.5 %copy.46 = bf16[1,65,65,1024]{3,2,1,0:T(8,128)(2,1)} copy(bf16[1,65,65,1024]{3,1,2,0:T(8,128)(2,1)} %get-tuple-element.6) | data formatting | bytes 17305600 | tf_op jit(solution)/shard_map/slice | solution.py:75
  516.7 10.5 %squeeze.17 = bf16[4225,1024]{1,0:T(8,128)(2,1)} reshape(bf16[1,65,65,1024]{3,2,1,0:T(8,128)(2,1)} %copy.46) | data formatting | bytes 17305600 | tf_op jit(solution)/shard_map/squeeze | solution.py:75
  527.2 11.7 %copy.47 = bf16[1024,4225]{1,0:T(8,128)(2,1)} copy(bf16[1024,4225]{0,1:T(8,128)(2,1)} %bitcast.170) | data formatting | bytes 17305600 | tf_op jit(solution)/shard_map/qs,qm->sm/dot_general | solution.py:74
  538.9 8.3 %fusion.48 = bf16[1,512,4,256]{3,1,2,0:T(8,128)(2,1)S(1)} fusion(bf16[4,256,4225]{2,1,0:T(8,128)(2,1)} %bitcast.173, s32[512]{0:T(512)S(1)} %copy-done.9), kind=kOutput, calls=%fused_computation.45 | convolution fusion | flops 4435084288 | bytes 9703424 | tf_op jit(solution)/shard_map/qs,qm->sm/dot_general | solution.py:74
  547.2 4.9 fusion.45
  554.0 55.0 %all_to_all.33 = bf16[2,512,4,256]{3,2,0,1:T(4,128)(2,1)S(1)} all-to-all(bf16[2,512,4,256]{3,2,0,1:T(4,128)(2,1)S(1)} %copy.49), channel_id=1, replica_groups=mesh['tg'=2,'pw'=16] {'tg','pw'}, dimensions={1} | all-to-all | bytes 4194304 | tf_op jit(solution)/shard_map/all_to_all | solution.py:130
  (49 shorter events, 30.3 us)
Async XLA Ops:
  0.0 1.0 copy-start
  3.7 14.4 %copy-start.7 = (f32[128,128,4]{1,2,0:T(4,128)S(1)}, f32[128,128,4]{1,2,0:T(4,128)}, u32[]{:S(2)}) copy-start(f32[128,128,4]{1,2,0:T(4,128)} %param.7) | copy-start | bytes 786436
  10.8 162.2 %all-to-all-start = ((bf16[2,16,128,256]{3,1,0,2:T(8,128)(2,1)}), bf16[2,16,128,256]{3,1,0,2:T(8,128)(2,1)S(1)}, u32[]{:S(2)}, u32[]{:S(2)}) async-start(bf16[2,16,128,256]{3,1,0,2:T(8,128)(2,1)} %copy.34), calls=%async_computation | async-start | bytes 4194304 | tf_op jit(solution)/shard_map/all_to_all | solution.py:124
  50.1 80.1 %copy-start.10 = (s32[16]{0:T(128)S(1)}, s32[16]{0:T(128)}, u32[]{:S(2)}) copy-start(s32[16]{0:T(128)} %param.6) | copy-start | bytes 196
  293.7 70.8 %copy-start.5 = (bf16[1,2,128,65]{2,3,0,1:T(8,128)(2,1)S(1)}, bf16[1,2,128,65]{2,3,0,1:T(8,128)(2,1)}, u32[]{:S(2)}) copy-start(bf16[1,2,128,65]{2,3,0,1:T(8,128)(2,1)} %get-tuple-element.13) | copy-start | bytes 99844
  293.7 70.8 %copy-start.6 = (bf16[1,2,128,65]{2,3,0,1:T(8,128)(2,1)S(1)}, bf16[1,2,128,65]{2,3,0,1:T(8,128)(2,1)}, u32[]{:S(2)}) copy-start(bf16[1,2,128,65]{2,3,0,1:T(8,128)(2,1)} %get-tuple-element.14) | copy-start | bytes 99844
  527.2 11.7 %copy-start.9 = (s32[512]{0:T(512)S(1)}, s32[512]{0:T(512)}, u32[]{:S(2)}) copy-start(s32[512]{0:T(512)} %get-tuple-element.17) | copy-start | bytes 6148
  538.9 8.3 %copy-start.2 = (bf16[1024,4225]{1,0:T(8,128)(2,1)S(1)}, bf16[1024,4225]{1,0:T(8,128)(2,1)}, u32[]{:S(2)}) copy-start(bf16[1024,4225]{1,0:T(8,128)(2,1)} %copy.47) | copy-start | bytes 25958404
  552.3 61.6 %copy-start.3 = (f32[1,2,128,128]{2,3,1,0:T(8,128)S(1)}, f32[1,2,128,128]{2,3,1,0:T(8,128)}, u32[]{:S(2)}) copy-start(f32[1,2,128,128]{2,3,1,0:T(8,128)} %get-tuple-element.9) | copy-start | bytes 393220
  552.3 61.6 %copy-start.4 = (f32[1,2,128,128]{2,3,1,0:T(8,128)S(1)}, f32[1,2,128,128]{2,3,1,0:T(8,128)}, u32[]{:S(2)}) copy-start(f32[1,2,128,128]{2,3,1,0:T(8,128)} %get-tuple-element.12) | copy-start | bytes 393220
  554.0 62.0 %copy-start.8 = (s32[256]{0:T(256)S(1)}, s32[256]{0:T(256)}, u32[]{:S(2)}) copy-start(s32[256]{0:T(256)} %param.5) | copy-start | bytes 3076
  609.0 11.6 %copy-start.1 = (f32[2,256,256]{2,1,0:T(8,128)S(1)}, f32[2,256,256]{2,1,0:T(8,128)}, u32[]{:S(2)}) copy-start(f32[2,256,256]{2,1,0:T(8,128)} %param.4) | copy-start | bytes 1572868
where the time goes:
time: 631 us; the launch traced here: 621 us
  matrix products  281 us (45%)
  local copies, waits for them, and re-layouts  233 us (37%)
  blocking collectives  95.7 us (15%)
  starting transfers between devices  7.32 us (1%)
    mul x2, local copies, waits for them, and re-layouts, plane_pass(): psi_field.reshape(2, NR, NR, plane_count, band_count)  105 us
    dot_general x2, matrix products, plane_pass(): jnp.einsum('dyk,yxm->dkxm', ahead[part_index], lattice, preferred_element...  81.3 us
    dot_general x1, matrix products, plane_pass(): jnp.einsum('cdxr,ckxm->drkm', ahead, partial_value, preferred_element_typ...  70.8 us
    dot_general x1, matrix products, plane_pass(): jnp.einsum('cdyq,cxym->dqxm', behind, weighted, preferred_element_type=jn...  65 us
    all_to_all x1, blocking collectives, body(): lax.all_to_all(returned, ('tg', 'pw'), split_axis=1, concat_axis=2, tiled...  55 us
    unnamed x1, blocking collectives  40.7 us
    slice x3, local copies, waits for them, and re-layouts, plane_pass(): boxed[part_index]  40 us
    dot_general x1, matrix products, plane_pass(): jnp.einsum('cdxq,cyxm->dqym', behind, reverse_half, preferred_element_typ...  24.8 us
  transfers between devices with their start and end apart: 1, of which 0 were waited for; matrix products, arithmetic and copies ran while one was open for 18% of the time, Pallas kernels for 0%

commit v1 on v0

--- a/solution.py
+++ b/solution.py
@@ -39,36 +39,32 @@
     return (ahead, behind)
 
 
-def plane_pass(received, selectors, volume, ahead, behind):
+def one_plane(flat, volume, selectors, ahead, behind):
     forward_select, backward_select = selectors
     box_side = ZSPAN + 1
-    plane_count = received.shape[2]
-    band_count = received.shape[3]
-    width = plane_count * band_count
-    flat = received.reshape(2, received.shape[1], width)
-    partial_value = None
-    for part_index in range(2):
-        lattice = jnp.dot(
-            forward_select, flat[part_index], preferred_element_type=jnp.float32
-        ).astype(jnp.bfloat16)
-        lattice = lattice.reshape(box_side, box_side, width)
-        term = jnp.einsum(
-            "dyk,yxm->dkxm", ahead[part_index], lattice, preferred_element_type=jnp.float32
-        )
-        partial_value = term if partial_value is None else partial_value + term
-    partial_value = partial_value.astype(jnp.bfloat16)
+    band_count = flat.shape[2]
+    lattice = jnp.stack(
+        [
+            jnp.dot(forward_select, flat[part_index], preferred_element_type=jnp.float32)
+            .astype(jnp.bfloat16)
+            .reshape(box_side, box_side, band_count)
+            for part_index in range(2)
+        ]
+    )
+    partial_value = jnp.einsum(
+        "cdyk,cyxm->dkxm", ahead, lattice, preferred_element_type=jnp.float32
+    ).astype(jnp.bfloat16)
     psi_field = jnp.einsum(
         "cdxr,ckxm->drkm", ahead, partial_value, preferred_element_type=jnp.float32
     )
-    psi_field = psi_field.reshape(2, NR, NR, plane_count, band_count) * volume[None, :, :, :, None]
-    weighted = psi_field.reshape(2, NR, NR, width).astype(jnp.bfloat16)
+    weighted = (psi_field * volume[None, :, :, None]).astype(jnp.bfloat16)
     reverse_half = jnp.einsum(
         "cdyq,cxym->dqxm", behind, weighted, preferred_element_type=jnp.float32
     ).astype(jnp.bfloat16)
     real_image = jnp.einsum(
         "cdxq,cyxm->dqym", behind, reverse_half, preferred_element_type=jnp.float32
     )
-    boxed = real_image.astype(jnp.bfloat16).reshape(2, box_side * box_side, width)
+    boxed = real_image.astype(jnp.bfloat16).reshape(2, box_side * box_side, band_count)
     picked = jnp.stack(
         [
             jnp.einsum(
@@ -77,7 +73,15 @@
             for part_index in range(2)
         ]
     )
-    return picked.astype(jnp.bfloat16).reshape(2, received.shape[1], plane_count, band_count)
+    return picked.astype(jnp.bfloat16)
+
+
+def plane_pass(received, selectors, volume, ahead, behind):
+    def step(carry, item):
+        return carry, one_plane(item[0], item[1], selectors, ahead, behind)
+
+    planes = (jnp.moveaxis(received, 2, 0), jnp.moveaxis(volume, 2, 0))
+    return jnp.moveaxis(lax.scan(step, None, planes)[1], 0, 2)
 
 
 def spread(shared, indices, slot_total):
@@ -113,7 +117,11 @@
 
 
 def body(coeffs, g_place, stick_column, potential):
-    columns = lax.all_gather(stick_column, ("tg", "pw"), axis=0, tiled=True)
+    owners = lax.axis_size(("tg", "pw"))
+    copies = jnp.broadcast_to(stick_column[None], (owners,) + stick_column.shape)
+    columns = lax.all_to_all(
+        copies, ("tg", "pw"), split_axis=0, concat_axis=0, tiled=True
+    ).reshape(-1)
     ahead, behind = box_tables()
     slot_width = stick_column.shape[0]
     plane_of = jnp.arange(NR, dtype=jnp.int32)

time: 631 us -> 551 us (0.87)
  matrix products: 281 us -> 176 us
  waiting for transfers between devices: 0.01 us -> 48.8 us
  blocking collectives: 95.7 us -> 52.3 us
  local copies, waits for them, and re-layouts: 233 us -> 248 us
    convert_element_type x0 -> x8, local copies, waits for them, and re-layouts: none -> 144 us  [the longest x4 93.8 us: one_plane(): weighted = (psi_field * volume[None, :, :, None]).astype(jnp.bfloat16)]
    dot_general x9 -> x32, matrix products: 269 us -> 164 us  [the longest x4 56.3 us: one_plane(): jnp.einsum('cdxr,ckxm->drkm', ahead, partial_value, preferred_element_typ...]
    mul x2 -> x8, local copies, waits for them, and re-layouts: 105 us -> 0.37 us  [one_plane(): weighted = (psi_field * volume[None, :, :, None]).astype(jnp.bfloat16)]
    all_to_all x1, waiting for transfers between devices: 0.01 us -> 48.8 us  [body(): lax.all_to_all(sticks, ('tg', 'pw'), split_axis=2, concat_axis=1, tiled=T...]
    unnamed x1 -> x0, blocking collectives: 40.7 us -> none
    slice x4 -> x12, local copies, waits for them, and re-layouts: 41.2 us -> 16.5 us  [one_plane(): boxed[part_index]]
    dot_general x2 -> x0, local copies, waits for them, and re-layouts: 23.5 us -> none  [plane_pass(): jnp.einsum('qs,qm->sm', backward_select, boxed[part_index], preferred_ele...]
    reshape x2 -> x17, local copies, waits for them, and re-layouts: 21 us -> 35.5 us  [the longest x16 35.4 us: one_plane(): jnp.stack([jnp.dot(forward_select, flat[part_index], preferred_element_ty...]
  transfers between devices with their start and end apart: 1 -> 2, of which waited for: 0 -> 1; matrix products, arithmetic and copies ran while one was open for 18% -> 2% of each run, Pallas kernels for 0% -> 0%
where the time goes in v1:
time: 551 us; the launch traced here: 545 us
  local copies, waits for them, and re-layouts  248 us (45%)
  matrix products  176 us (32%)
  blocking collectives  52.3 us (9%)
  waiting for transfers between devices  48.8 us (9%)
  starting transfers between devices  13.2 us (2%)
  other arithmetic  6.07 us (1%)
    convert_element_type x4, local copies, waits for them, and re-layouts, one_plane(): weighted = (psi_field * volume[None, :, :, None]).astype(jnp.bfloat16)  93.8 us
    dot_general x4, matrix products, one_plane(): jnp.einsum('cdxr,ckxm->drkm', ahead, partial_value, preferred_element_typ...  56.3 us
    all_to_all x1, blocking collectives, body(): lax.all_to_all(returned, ('tg', 'pw'), split_axis=1, concat_axis=2, tiled...  52.3 us
    convert_element_type x4, local copies, waits for them, and re-layouts, one_plane(): partial_value = jnp.einsum('cdyk,cyxm->dkxm', ahead, lattice, preferred_e...  50.1 us
    all_to_all x1, waiting for transfers between devices, body(): lax.all_to_all(sticks, ('tg', 'pw'), split_axis=2, concat_axis=1, tiled=T...  48.8 us
    reshape x16, local copies, waits for them, and re-layouts, one_plane(): jnp.stack([jnp.dot(forward_select, flat[part_index], preferred_element_ty...  35.4 us
    squeeze x8, local copies, waits for them, and re-layouts, one_plane(): boxed[part_index]  30.5 us
    dot_general x4, matrix products, one_plane(): jnp.einsum('cdyq,cxym->dqxm', behind, weighted, preferred_element_type=jn...  28.7 us
  transfers between devices with their start and end apart: 2, of which 1 were waited for; matrix products, arithmetic and copies ran while one was open for 2% of the time, Pallas kernels for 0%

profile of v1, /device:TPU:0, one launch (start us, length us, event | category | flops | bytes accessed | tf_op | source)
XLA Modules:
  0.0 544.8 jit_solution(8175627262599642719)
XLA Ops:
  1.3 7.3 %all-to-all-start.1 = ((s32[32,1,16]{2,1,0:T(1,128)}), s32[32,1,16]{2,1,0:T(1,128)S(1)}, u32[]{:S(2)}, u32[]{:S(2)}) async-start(s32[32,1,16]{2,1,0:T(1,128)} %broadcast_in_dim.6), calls=%async_computation.1 | async-start | bytes 32768 | tf_op jit(solution)/shard_map/all_to_all | solution.py:122
  19.3 5.8 %all-to-all-start = ((bf16[2,16,128,256]{3,1,0,2:T(8,128)(2,1)}), bf16[2,16,128,256]{3,1,0,2:T(8,128)(2,1)S(1)}, u32[]{:S(2)}, u32[]{:S(2)}) async-start(bf16[2,16,128,256]{3,1,0,2:T(8,128)(2,1)} %copy.40), calls=%async_computation | async-start | bytes 4194304 | tf_op jit(solution)/shard_map/all_to_all | solution.py:132
  27.0 48.8 %all-to-all-done = bf16[2,16,128,256]{3,1,0,2:T(8,128)(2,1)S(1)} async-done(((bf16[2,16,128,256]{3,1,0,2:T(8,128)(2,1)}), bf16[2,16,128,256]{3,1,0,2:T(8,128)(2,1)S(1)}, u32[]{:S(2)}, u32[]{:S(2)}) %all-to-all-start) | async-done | bytes 2097184 | tf_op jit(solution)/shard_map/all_to_all | solution.py:132
  77.2 399.3 %while.11 = (s32[]{:T(128)}, bf16[4,2,512,256]{2,3,1,0:T(8,128)(2,1)}, bf16[4,2,512,256]{3,2,1,0:T(8,128)(2,1)}, bf16[2,2,65,128]{3,2,0,1:T(8,128)(2,1)S(1)}, f3...) while((s32[]{:T(128)}, ...), condition=%wide.region_1.2_spmd.clone, body=%wide.region_0.1_spmd.clone.sunk | while | flops 11064318976 | bytes 190150320 | solution.py:84
  94.5 4.9 fusion.150
  99.3 12.5 %copy.100 = bf16[2,128,65,256,1]{3,2,0,4,1:T(8,128)(2,1)} copy(bf16[2,128,65,256,1]{1,3,0,2,4:T(8,128)(2,1)} %fusion.150) | data formatting | bytes 17039360 | tf_op jit(solution)/shard_map/while/body/eval_jaxpr/convert_element_type | solution.py:56
  112.0 14.1 %fusion.151 = bf16[2,128,128,256,1]{1,3,0,2,4:T(8,128)(2,1)} fusion(f32[128,128]{0,1:T(8,128)S(1)} %copy.97, bf16[2,128,65,256,1]{3,2,0,4,1:T(8,128)(2,1)} %copy.100, bf16[2,2,65,128]{3,2,0,1:T(8,128)(2,1)S(1)} %get-tuple-element.185), kind=kOutput, calls=%fused_computation.6.clone.1 | convolution fusion | flops 2197815296 | bytes 25428992 | tf_op jit(solution)/shard_map/while/body/eval_jaxpr/cdxr,ckxm->drkm/dot_general | solution.py:57
  126.0 23.5 %copy.101 = bf16[2,128,128,256,1]{3,2,0,4,1:T(8,128)(2,1)} copy(bf16[2,128,128,256,1]{1,3,0,2,4:T(8,128)(2,1)} %fusion.151) | data formatting | bytes 33554432 | tf_op jit(solution)/shard_map/while/body/eval_jaxpr/convert_element_type | solution.py:60
  149.5 7.2 %fusion.152 = bf16[2,65,128,256,1]{3,1,0,2,4:T(8,128)(2,1)S(1)} fusion(bf16[2,128,128,256,1]{3,2,0,4,1:T(8,128)(2,1)} %copy.101, bf16[2,2,128,65]{2,3,0,1:T(8,128)(2,1)S(1)} %get-tuple-element.187), kind=kOutput, calls=%fused_computation.8.clone.1 | convolution fusion | flops 2185297920 | bytes 25363456 | tf_op jit(solution)/shard_map/while/body/eval_jaxpr/cdyq,cxym->dqxm/dot_general | solution.py:61
  194.3 4.9 fusion.150
  199.1 12.5 %copy.100 = bf16[2,128,65,256,1]{3,2,0,4,1:T(8,128)(2,1)} copy(bf16[2,128,65,256,1]{1,3,0,2,4:T(8,128)(2,1)} %fusion.150) | data formatting | bytes 17039360 | tf_op jit(solution)/shard_map/while/body/eval_jaxpr/convert_element_type | solution.py:56
  211.8 14.1 %fusion.151 = bf16[2,128,128,256,1]{1,3,0,2,4:T(8,128)(2,1)} fusion(f32[128,128]{0,1:T(8,128)S(1)} %copy.97, bf16[2,128,65,256,1]{3,2,0,4,1:T(8,128)(2,1)} %copy.100, bf16[2,2,65,128]{3,2,0,1:T(8,128)(2,1)S(1)} %get-tuple-element.185), kind=kOutput, calls=%fused_computation.6.clone.1 | convolution fusion | flops 2197815296 | bytes 25428992 | tf_op jit(solution)/shard_map/while/body/eval_jaxpr/cdxr,ckxm->drkm/dot_general | solution.py:57
  225.8 23.5 %copy.101 = bf16[2,128,128,256,1]{3,2,0,4,1:T(8,128)(2,1)} copy(bf16[2,128,128,256,1]{1,3,0,2,4:T(8,128)(2,1)} %fusion.151) | data formatting | bytes 33554432 | tf_op jit(solution)/shard_map/while/body/eval_jaxpr/convert_element_type | solution.py:60
  249.3 7.2 %fusion.152 = bf16[2,65,128,256,1]{3,1,0,2,4:T(8,128)(2,1)S(1)} fusion(bf16[2,128,128,256,1]{3,2,0,4,1:T(8,128)(2,1)} %copy.101, bf16[2,2,128,65]{2,3,0,1:T(8,128)(2,1)S(1)} %get-tuple-element.187), kind=kOutput, calls=%fused_computation.8.clone.1 | convolution fusion | flops 2185297920 | bytes 25363456 | tf_op jit(solution)/shard_map/while/body/eval_jaxpr/cdyq,cxym->dqxm/dot_general | solution.py:61
  294.1 4.9 fusion.150
  298.9 12.5 %copy.100 = bf16[2,128,65,256,1]{3,2,0,4,1:T(8,128)(2,1)} copy(bf16[2,128,65,256,1]{1,3,0,2,4:T(8,128)(2,1)} %fusion.150) | data formatting | bytes 17039360 | tf_op jit(solution)/shard_map/while/body/eval_jaxpr/convert_element_type | solution.py:56
  311.6 14.1 %fusion.151 = bf16[2,128,128,256,1]{1,3,0,2,4:T(8,128)(2,1)} fusion(f32[128,128]{0,1:T(8,128)S(1)} %copy.97, bf16[2,128,65,256,1]{3,2,0,4,1:T(8,128)(2,1)} %copy.100, bf16[2,2,65,128]{3,2,0,1:T(8,128)(2,1)S(1)} %get-tuple-element.185), kind=kOutput, calls=%fused_computation.6.clone.1 | convolution fusion | flops 2197815296 | bytes 25428992 | tf_op jit(solution)/shard_map/while/body/eval_jaxpr/cdxr,ckxm->drkm/dot_general | solution.py:57
  325.6 23.5 %copy.101 = bf16[2,128,128,256,1]{3,2,0,4,1:T(8,128)(2,1)} copy(bf16[2,128,128,256,1]{1,3,0,2,4:T(8,128)(2,1)} %fusion.151) | data formatting | bytes 33554432 | tf_op jit(solution)/shard_map/while/body/eval_jaxpr/convert_element_type | solution.py:60
  349.1 7.2 %fusion.152 = bf16[2,65,128,256,1]{3,1,0,2,4:T(8,128)(2,1)S(1)} fusion(bf16[2,128,128,256,1]{3,2,0,4,1:T(8,128)(2,1)} %copy.101, bf16[2,2,128,65]{2,3,0,1:T(8,128)(2,1)S(1)} %get-tuple-element.187), kind=kOutput, calls=%fused_computation.8.clone.1 | convolution fusion | flops 2185297920 | bytes 25363456 | tf_op jit(solution)/shard_map/while/body/eval_jaxpr/cdyq,cxym->dqxm/dot_general | solution.py:61
  398.8 12.5 %copy.100 = bf16[2,128,65,256,1]{3,2,0,4,1:T(8,128)(2,1)} copy(bf16[2,128,65,256,1]{1,3,0,2,4:T(8,128)(2,1)} %fusion.150) | data formatting | bytes 17039360 | tf_op jit(solution)/shard_map/while/body/eval_jaxpr/convert_element_type | solution.py:56
  411.4 14.1 %fusion.151 = bf16[2,128,128,256,1]{1,3,0,2,4:T(8,128)(2,1)} fusion(f32[128,128]{0,1:T(8,128)S(1)} %copy.97, bf16[2,128,65,256,1]{3,2,0,4,1:T(8,128)(2,1)} %copy.100, bf16[2,2,65,128]{3,2,0,1:T(8,128)(2,1)S(1)} %get-tuple-element.185), kind=kOutput, calls=%fused_computation.6.clone.1 | convolution fusion | flops 2197815296 | bytes 25428992 | tf_op jit(solution)/shard_map/while/body/eval_jaxpr/cdxr,ckxm->drkm/dot_general | solution.py:57
  425.5 23.5 %copy.101 = bf16[2,128,128,256,1]{3,2,0,4,1:T(8,128)(2,1)} copy(bf16[2,128,128,256,1]{1,3,0,2,4:T(8,128)(2,1)} %fusion.151) | data formatting | bytes 33554432 | tf_op jit(solution)/shard_map/while/body/eval_jaxpr/convert_element_type | solution.py:60
  448.9 7.2 %fusion.152 = bf16[2,65,128,256,1]{3,1,0,2,4:T(8,128)(2,1)S(1)} fusion(bf16[2,128,128,256,1]{3,2,0,4,1:T(8,128)(2,1)} %copy.101, bf16[2,2,128,65]{2,3,0,1:T(8,128)(2,1)S(1)} %get-tuple-element.187), kind=kOutput, calls=%fused_computation.8.clone.1 | convolution fusion | flops 2185297920 | bytes 25363456 | tf_op jit(solution)/shard_map/while/body/eval_jaxpr/cdyq,cxym->dqxm/dot_general | solution.py:61
  480.0 52.3 %all_to_all.42 = bf16[2,512,4,256]{3,2,0,1:T(4,128)(2,1)S(1)} all-to-all(bf16[2,512,4,256]{3,2,0,1:T(4,128)(2,1)S(1)} %bitcast.207), channel_id=1, replica_groups=mesh['tg'=2,'pw'=16] {'tg','pw'}, dimensions={1} | all-to-all | bytes 4194304 | tf_op jit(solution)/shard_map/all_to_all | solution.py:138
  (119 shorter events, 186.7 us)
Async XLA Ops:
  0.0 9.5 %copy-start = (f32[2,256,256]{2,1,0:T(8,128)S(1)}, f32[2,256,256]{2,1,0:T(8,128)}, u32[]{:S(2)}) copy-start(f32[2,256,256]{2,1,0:T(8,128)} %param.6) | copy-start | bytes 1572868
  1.3 18.0 %all-to-all-start.1 = ((s32[32,1,16]{2,1,0:T(1,128)}), s32[32,1,16]{2,1,0:T(1,128)S(1)}, u32[]{:S(2)}, u32[]{:S(2)}) async-start(s32[32,1,16]{2,1,0:T(1,128)} %broadcast_in_dim.6), calls=%async_computation.1 | async-start | bytes 32768 | tf_op jit(solution)/shard_map/all_to_all | solution.py:122
  16.7 8.4 %copy-start.5 = (f32[128,128,4]{1,2,0:T(4,128)S(1)}, f32[128,128,4]{1,2,0:T(4,128)}, u32[]{:S(2)}) copy-start(f32[128,128,4]{1,2,0:T(4,128)} %param.9) | copy-start | bytes 786436
  19.3 56.4 %all-to-all-start = ((bf16[2,16,128,256]{3,1,0,2:T(8,128)(2,1)}), bf16[2,16,128,256]{3,1,0,2:T(8,128)(2,1)S(1)}, u32[]{:S(2)}, u32[]{:S(2)}) async-start(bf16[2,16,128,256]{3,1,0,2:T(8,128)(2,1)} %copy.40), calls=%async_computation | async-start | bytes 4194304 | tf_op jit(solution)/shard_map/all_to_all | solution.py:132
  92.8 1.7 copy-start.2
  192.6 1.7 copy-start.2
  292.4 1.7 copy-start.2
  392.3 1.7 copy-start.2
  532.6 5.5 %copy-start.3 = (f32[1,2,128,128]{2,3,1,0:T(8,128)S(1)}, f32[1,2,128,128]{2,3,1,0:T(8,128)}, u32[]{:S(2)}) copy-start(f32[1,2,128,128]{2,3,1,0:T(8,128)} %get-tuple-element.87) | copy-start | bytes 393220
  532.6 5.5 %copy-start.4 = (f32[1,2,128,128]{2,3,1,0:T(8,128)S(1)}, f32[1,2,128,128]{2,3,1,0:T(8,128)}, u32[]{:S(2)}) copy-start(f32[1,2,128,128]{2,3,1,0:T(8,128)} %get-tuple-element.90) | copy-start | bytes 393220
  538.2 2.0 copy-start.6
  538.2 6.6 %copy-start.1 = (f32[2,256,256]{2,1,0:T(8,128)S(1)}, f32[2,256,256]{2,1,0:T(8,128)}, u32[]{:S(2)}) copy-start(f32[2,256,256]{2,1,0:T(8,128)} %param.6) | copy-start | bytes 1572868
